TPU v7x, 128 devices: a whole 4x4x4 slice. The times are simulated.
128 devices in a mesh: row: 8 (over x, z_lo), col: 16 (over y, z_hi, core).
Axes of the slice: x: 4, y: 4, z: 4 (z_hi: 2, z_lo: 2; z = z_hi * 2 + z_lo), core: 2. Of those that a mesh axis runs over, the one named last changes fastest.
Arguments:
- momentum: bfloat16 [16384, 16384], P('row', 'col'), may hold values from -6 to 6
- gradient: bfloat16 [16384, 16384], P('row', 'col'), may hold values from -43 to 43
- right_prev: float32 [16384, 512], P('col'), may hold values from -6 to 6
- weight: bfloat16 [16384, 16384], P('col', 'row'), may hold values from -0.046875 to 0.046875
- tokens: bfloat16 [256, 16384], P(None, 'row'), may hold values from -6 to 6
Outputs:
- new_momentum: bfloat16 [16384, 16384], P('row', 'col')
- new_basis: float32 [16384, 512], P('col')
- new_weight: bfloat16 [16384, 16384], P('col', 'row')
- projected: bfloat16 [256, 16384], P('row', 'col')
All inputs are finite; a program needn't handle non-finite values.
Results may differ from a plain program's by a relative error of at most 0.006.
Values may be sent and summed in bfloat16 or wider, within the bound.
No kernel may reach another device: no remote copies, remote signals or barrier semaphores. Data moves between devices by JAX's collectives and lax.ppermute only.
A program may use at most 128 MiB of HBM per device.

v0:
```python
import functools

import jax
import jax.numpy as jnp
from jax import lax
from jax.sharding import Mesh
from jax.sharding import PartitionSpec as P

DIN = 16384
COL = ("col_0", "col_1", "col_2")
ROW = ("row_0", "row_1")
ROW_COL = ("row_0", "row_1", "col_0", "col_1", "col_2")


decay_part = 0.05
step_size = 0.01
epsilon = 1e-06


def cut_along(array, dim, length):
    shape = array.shape
    pieces = array.reshape(*shape[:dim], length, shape[dim] // length, *shape[dim + 1 :])
    return jnp.moveaxis(pieces, dim, 0)


def summed_on_arrival(array, axis, dim):
    length = lax.axis_size(axis)
    pieces = lax.all_to_all(cut_along(array, dim, length), axis, 0, 0, tiled=True)
    return jnp.sum(pieces, axis=0)


def over_axes(array, axes):
    return functools.reduce(lax.psum, axes, array)


def joined_along(pieces, dim):
    pieces = jnp.moveaxis(pieces, 0, dim)
    shape = pieces.shape
    return pieces.reshape(*shape[:dim], shape[dim] * shape[dim + 1], *shape[dim + 2 :])


def from_everyone(array, axis):
    length = lax.axis_size(axis)
    return lax.all_to_all(
        jnp.broadcast_to(array[None], (length, *array.shape)), axis, 0, 0, tiled=True
    )


def collect(array, axis, dim):
    return joined_along(from_everyone(array, axis), dim)


def filled_up(lines, length):
    spare = -len(lines) % length
    return jnp.pad(lines, [(0, spare)] + [(0, 0)] * (lines.ndim - 1))


def spread(array, axis, root):
    lines = jnp.where(lax.axis_index(axis) == root, array, jnp.zeros_like(array)).reshape(
        -1, *array.shape[1:][-1:]
    )
    padded = filled_up(lines, lax.axis_size(axis))
    own = lax.psum_scatter(padded, axis, scatter_dimension=0, tiled=True)
    return lax.all_gather(own, axis, axis=0, tiled=True)[: len(lines)].reshape(array.shape)


def from_root(array, axis, root):
    return lax.dynamic_index_in_dim(lax.all_gather(array, axis), root, 0, keepdims=False)


def contract_first(lhs, rhs, highest):
    return lax.dot_general(
        lhs, rhs, (((0,), (0,)), ((), ())), precision=highest, preferred_element_type=jnp.float32
    )


def contract_last(lhs, rhs, highest):
    return lax.dot_general(
        lhs, rhs, (((1,), (1,)), ((), ())), precision=highest, preferred_element_type=jnp.float32
    )


def per_device(momentum, gradient, right_prev, weight, tokens):
    highest = lax.Precision.HIGHEST
    mixed = momentum.astype(jnp.float32) + gradient.astype(jnp.float32)
    partial_left = jnp.dot(mixed, right_prev, precision=highest, preferred_element_type=jnp.float32)
    left_raw = lax.psum(partial_left, COL)
    gram_matrix = lax.psum(contract_first(left_raw, left_raw, highest), ROW)
    factor = jnp.linalg.cholesky(gram_matrix)
    left_factor = lax.linalg.triangular_solve(
        factor, left_raw, left_side=False, lower=True, transpose_a=True
    )
    partial_right = contract_first(mixed, left_factor, highest)
    right_shard = summed_on_arrival(partial_right, ROW, 0)
    squares = over_axes(jnp.sum(right_shard * right_shard, axis=0), ROW_COL)
    right_factor = collect(right_shard, ROW, 0)
    new_basis = right_factor * lax.rsqrt(squares / DIN + epsilon)
    outer = contract_last(left_factor, right_factor, highest)
    new_momentum = (mixed - decay_part * outer).astype(jnp.bfloat16)
    span_count = lax.axis_size(COL) // lax.axis_size(ROW)
    col_index = lax.axis_index(COL)
    row_index = lax.axis_index(ROW)
    block_rows = left_factor.shape[0] // span_count
    own_block = lax.dynamic_slice_in_dim(
        left_factor, col_index % span_count * block_rows, block_rows, 0
    )
    left_tile = spread(own_block.astype(jnp.bfloat16), ROW, col_index // span_count)
    basis_send = new_basis.astype(jnp.bfloat16)
    pieces = [
        from_root(basis_send, COL, row_index * span_count + piece_index)
        for piece_index in range(span_count)
    ]
    basis_tile = jnp.concatenate(pieces, axis=0)
    update = lax.dot_general(
        left_tile, basis_tile, (((1,), (1,)), ((), ())), preferred_element_type=jnp.float32
    )
    new_weight = (weight.astype(jnp.float32) - step_size * update).astype(jnp.bfloat16)
    projected = summed_on_arrival(
        lax.dot_general(
            tokens, new_weight, (((1,), (1,)), ((), ())), preferred_element_type=jnp.float32
        ),
        ROW,
        0,
    ).astype(jnp.bfloat16)
    return (new_momentum, new_basis, new_weight, projected)


def solution(mesh):
    torus = Mesh(mesh.devices.reshape(4, 2, 4, 2, 2), ("row_0", "row_1", "col_0", "col_1", "col_2"))
    placed = (P(ROW, COL), P(ROW, COL), P(COL, None), P(COL, ROW), P(None, ROW))
    return jax.shard_map(
        per_device,
        mesh=torus,
        in_specs=placed,
        out_specs=(P(ROW, COL), P(COL, None), P(COL, ROW), P(ROW, COL)),
        check_vma=False,
    )
```

profile of v0, /device:TPU:2, one launch (start us, length us, event | category | flops | bytes accessed | tf_op | source)
XLA Modules:
  0.0 745.4 jit_solution(4212846563401317149)
XLA Ops:
  7.2 1.5 copy-done
  8.8 17.3 %fusion.1 = f32[2048,512]{1,0:T(8,128)} fusion(f32[1024,512]{1,0:T(8,128)S(1)} %copy-done, bf16[2048,1024]{1,0:T(8,128)(2,1)} %param.6, bf16[2048,1024]{1,0:T(8,128)(2,1)} %param.5), kind=kOutput, calls=%fused_computation.6 | convolution fusion | flops 12891193344 | bytes 14680064 | tf_op jit(solution)/shard_map/dot_general | solution.py:86
  26.2 154.4 %all-reduce.4.cloned.1.call-done = f32[2048,512]{1,0:T(8,128)} async-done(((f32[2048,512]{1,0:T(8,128)}), f32[2048,512]{1,0:T(8,128)}) %all-reduce.4.cloned.1.call-update) | async-done | bytes 4194320 | tf_op jit(solution)/shard_map/psum | solution.py:87
  180.6 11.6 %fusion.43 = f32[512,512]{0,1:T(8,128)} fusion(f32[2048,512]{1,0:T(8,128)} %all-reduce.4.cloned.1.call-done), kind=kOutput, calls=%fused_computation.86 | convolution fusion | flops 6442450944 | bytes 5242880 | tf_op jit(solution)/shard_map/dot_general | solution.py:72
  192.2 76.7 %all-reduce.6.cloned.1.call-done = f32[512,512]{0,1:T(8,128)} async-done(((f32[512,512]{0,1:T(8,128)}), f32[512,512]{0,1:T(8,128)}) %all-reduce.6.cloned.1.call-update) | async-done | bytes 1048592 | tf_op jit(solution)/shard_map/psum | solution.py:88
  268.8 1.6 copy.12
  270.4 1.4 fusion.21
  271.9 11.7 %cholesky.104 = f32[128,128]{1,0:T(8,128)S(1)} custom-call(f32[128,128]{1,0:T(8,128)S(1)} %cholesky.266), custom_call_target="Cholesky" | custom-call | tf_op jit(solution)/shard_map/jit(cholesky)/cholesky | solution.py:89
  283.6 9.8 %custom-call.30 = f32[1,128,128]{1,2,0:T(8,128)S(1)} custom-call(f32[1,128,128]{2,1,0:T(8,128)S(1)} %get-tuple-element.33), custom_call_target="InvertDiagBlocksLowerTriangular" | custom-call | tf_op jit(solution)/shard_map/jit(cholesky)/cholesky | solution.py:89
  293.6 0.3 constant_dynamic-update-slice_fusion.1
  293.9 0.3 convolution_subtract_fusion.2
  294.2 11.7 %cholesky.217 = f32[128,128]{1,0:T(8,128)S(1)} custom-call(f32[128,128]{1,0:T(8,128)S(1)} %cholesky.270), custom_call_target="Cholesky" | custom-call | tf_op jit(solution)/shard_map/jit(cholesky)/cholesky | solution.py:89
  306.0 10.2 %custom-call.31 = f32[1,128,128]{1,2,0:T(8,128)S(1)} custom-call(f32[1,128,128]{2,1,0:T(8,128)S(1)} %get-tuple-element.30), custom_call_target="InvertDiagBlocksLowerTriangular" | custom-call | tf_op jit(solution)/shard_map/jit(cholesky)/cholesky | solution.py:89
  316.4 0.4 convolution_subtract_fusion.3
  316.8 11.7 %cholesky.238 = f32[128,128]{1,0:T(8,128)S(1)} custom-call(f32[128,128]{1,0:T(8,128)S(1)} %cholesky.275), custom_call_target="Cholesky" | custom-call | tf_op jit(solution)/shard_map/jit(cholesky)/cholesky | solution.py:89
  328.6 0.6 compare_reduce_fusion.1
  329.2 9.8 %custom-call.32 = f32[1,128,128]{1,2,0:T(8,128)S(1)} custom-call(f32[1,128,128]{2,1,0:T(8,128)S(1)} %get-tuple-element.27), custom_call_target="InvertDiagBlocksLowerTriangular" | custom-call | tf_op jit(solution)/shard_map/jit(cholesky)/cholesky | solution.py:89
  339.3 0.4 convolution_subtract_fusion.4
  339.7 11.7 %cholesky.255 = f32[128,128]{1,0:T(8,128)S(1)} custom-call(f32[128,128]{1,0:T(8,128)S(1)} %convolution_subtract_fusion.4), custom_call_target="Cholesky" | custom-call | tf_op jit(solution)/shard_map/jit(cholesky)/cholesky | solution.py:89
  351.4 0.7 compare_reduce_fusion
  352.1 0.6 compare_reduce_fusion.2
  355.3 0.3 select_select_fusion
  355.6 8.0 %while.1 = (s32[]{:T(128)}, f32[512,512]{1,0:T(8,128)S(1)}, s32[4,2]{0,1:T(2,128)S(1)}, f32[4,128,128]{2,1,0:T(8,128)S(1)}, s32[]{:T(128)}) while((s32[]{:T(128)}, f32[512,512]{1,0:T(8,128)S(1)}, s32[4,2]{0,1:T(2,128)S(1)}, f32[4,128,128]{2,1,0:T(8,128)S(1)}, s32[]{:T(128)}) %tuple.32), condition=%wide.while_cond, body=%wide.while_body.sunk | while | flops 2 | bytes 131189 | solution.py:90
  355.7 0.5 fusion.58
  356.2 1.4 bitcast_dynamic-update-slice_fusion.2
  357.7 0.5 fusion.58
  358.2 1.4 bitcast_dynamic-update-slice_fusion.2
  359.7 0.5 fusion.58
  360.2 1.4 bitcast_dynamic-update-slice_fusion.2
  361.7 0.5 fusion.58
  362.2 1.4 bitcast_dynamic-update-slice_fusion.2
  363.6 39.3 %custom-call.33 = f32[4,128,128]{1,2,0:T(8,128)S(1)} custom-call(f32[4,128,128]{2,1,0:T(8,128)S(1)} %get-tuple-element.11), custom_call_target="InvertDiagBlocksLowerTriangular" | custom-call | tf_op jit(solution)/shard_map/triangular_solve | solution.py:90
  402.9 2.5 fusion.19
  405.4 3.1 convolution_subtract_fusion.1
  408.5 1.1 fusion.32
  409.6 4.6 convolution_subtract_fusion
  414.2 1.1 fusion.31
  415.3 7.2 fusion.8
  422.6 1.1 fusion.30
  423.7 27.9 %fusion = f32[1024,512]{1,0:T(8,128)} fusion(bf16[2048,1024]{1,0:T(8,128)(2,1)S(1)} %copy-done.8, bf16[2048,1024]{1,0:T(8,128)(2,1)S(1)} %copy-done.9, f32[2048,128]{0,1:T(8,128)S(1)} %fusion.30, f32[2048,128]{0,1:T(8,128)S(1)} %fusion.31, f32[2048,128]{0,1:T(8,128)S(1)} %fusion.32, f32[2048,128]{0,1:T(8,128)S(1)} %fusion.19), kind=kOutput, calls=%fused_computation.5 | convolution fusion | flops 12894339072 | bytes 14680064 | tf_op jit(solution)/shard_map/dot_general | solution.py:72
  451.6 6.1 all-to-all-start
  457.8 2.9 pad_maximum_fusion
  460.6 20.1 %all-to-all-done = f32[8,128,512]{2,1,0:T(8,128)} async-done(((f32[8,128,512]{2,1,0:T(8,128)}), f32[8,128,512]{2,1,0:T(8,128)}, u32[]{:S(2)}, u32[]{:S(2)}) %all-to-all-start) | async-done | bytes 2097184 | tf_op jit(solution)/shard_map/all_to_all | solution.py:28
  480.8 1.8 reduce_sum.27
  482.6 1.6 broadcast_in_dim.6
  484.2 5.7 all-to-all-start.1
  489.9 2.4 fusion.18
  492.3 2.3 copy.14
  494.7 21.3 %psum.51 = f32[512]{0:T(512)S(1)} all-reduce(f32[512]{0:T(512)S(1)} %multiply_reduce_fusion), channel_id=1, replica_groups=mesh['row_0'=4,'row_1'=2,'col_0'=4,'col_1'=2,'col_2'=2] {'row_0'}, use_global_device_ids=true, to_apply=%region_12.13 | all-reduce | flops 512 | bytes 4096 | tf_op jit(solution)/shard_map/psum | solution.py:33
  516.1 5.2 psum.52
  521.3 10.5 %psum.53 = f32[512]{0:T(512)S(1)} all-reduce(f32[512]{0:T(512)S(1)} %psum.52), channel_id=1, replica_groups=mesh['row_0'=4,'row_1'=2,'col_0'=4,'col_1'=2,'col_2'=2] {'col_0'}, use_global_device_ids=true, to_apply=%region_14.15 | all-reduce | flops 512 | bytes 4096 | tf_op jit(solution)/shard_map/psum | solution.py:33
  531.8 6.4 psum.54
  538.2 2.4 psum.55
  540.7 1.4 fusion.17
  542.2 1.7 copy.15
  543.9 1.6 broadcast_multiply_fusion
  545.5 105.9 %all-gather.5.cloned.1.call-done = bf16[16,1024,512]{2,1,0:T(8,128)(2,1)} async-done(((bf16[1,1024,512]{2,1,0:T(8,128)(2,1)}), bf16[16,1024,512]{2,1,0:T(8,128)(2,1)}) %all-gather.5.cloned.1.call-update) | async-done | bytes 16777232 | tf_op jit(solution)/shard_map/all_gather | solution.py:68
  651.4 1.7 dynamic-slice_bitcast_fusion.1
  653.1 37.1 %all-gather.3.cloned.1.call-done = bf16[1024,512]{0,1:T(8,128)(2,1)} async-done(((bf16[128,512]{0,1:T(8,128)(2,1)}), bf16[1024,512]{0,1:T(8,128)(2,1)}) %all-gather.3.cloned.1.call-update) | async-done | bytes 1048592 | tf_op jit(solution)/shard_map/all_gather | solution.py:64
  690.2 5.0 subtract_convert_fusion
  695.2 2.4 fusion.44
  697.6 7.8 %all-to-all-start.2 = ((f32[8,32,1024]{2,1,0:T(8,128)}), f32[8,32,1024]{2,1,0:T(8,128)}, u32[]{:S(2)}, u32[]{:S(2)}) async-start(f32[8,32,1024]{2,1,0:T(8,128)} %bitcast.17), calls=%async_computation.2 | async-start | bytes 2097152 | tf_op jit(solution)/shard_map/all_to_all | solution.py:28
  705.4 31.3 %subtract_convert_fusion.1 = bf16[2048,1024]{1,0:T(8,128)(2,1)} fusion(bf16[2048,1024]{1,0:T(8,128)(2,1)} %param.6, bf16[2048,1024]{1,0:T(8,128)(2,1)} %param.5, f32[1024,512]{1,0:T(8,128)} %bitcast.72, f32[2048,128]{0,1:T(8,128)} %copy-done.6, f32[2048,128]{0,1:T(8,128)} %copy-done.5, f32[2048,128]{0,1:T(8,128)} %copy-done.4, f32[2048,128]{0,1:T(8,128)S(1)} %fusion.19), kind=kOutput, calls=%fused_computation.3 | convolution fusion | flops 12900630528 | bytes 18874368 | tf_op jit(solution)/shard_map/dot_general | solution.py:78
  736.8 1.9 reduce_sum.29
  (55 shorter events, 1.4 us)
Async XLA Ops:
  7.2 1.6 copy-start
  7.2 173.4 %all-reduce.4.cloned.1.call-start = ((), (), s32[]{:S(2)}) async-start(), calls=%async_computation.4 | async-start | bytes 8388608 | tf_op jit(solution)/shard_map/psum | solution.py:87
  26.1 242.7 %all-reduce.6.cloned.1.call-start = ((), (), s32[]{:S(2)}) async-start(), calls=%async_computation.5 | async-start | bytes 2097152 | tf_op jit(solution)/shard_map/psum | solution.py:88
  363.6 39.3 %copy-start.7 = (f32[512,512]{1,0:T(8,128)}, f32[512,512]{1,0:T(8,128)S(1)}, u32[]{:S(2)}) copy-start(f32[512,512]{1,0:T(8,128)S(1)} %get-tuple-element.100) | copy-start | bytes 3145732
  402.9 6.6 copy-start.2
  409.6 48.2 %copy-start.4 = (f32[2048,128]{0,1:T(8,128)}, f32[2048,128]{0,1:T(8,128)S(1)}, u32[]{:S(2)}) copy-start(f32[2048,128]{0,1:T(8,128)S(1)} %fusion.32) | copy-start | bytes 3145732
  414.2 9.5 %copy-start.9 = (bf16[2048,1024]{1,0:T(8,128)(2,1)S(1)}, bf16[2048,1024]{1,0:T(8,128)(2,1)}, u32[]{:S(2)}) copy-start(bf16[2048,1024]{1,0:T(8,128)(2,1)} %param.5) | copy-start | bytes 12582916
  415.3 42.5 %copy-start.5 = (f32[2048,128]{0,1:T(8,128)}, f32[2048,128]{0,1:T(8,128)S(1)}, u32[]{:S(2)}) copy-start(f32[2048,128]{0,1:T(8,128)S(1)} %fusion.31) | copy-start | bytes 3145732
  415.3 8.4 %copy-start.8 = (bf16[2048,1024]{1,0:T(8,128)(2,1)S(1)}, bf16[2048,1024]{1,0:T(8,128)(2,1)}, u32[]{:S(2)}) copy-start(bf16[2048,1024]{1,0:T(8,128)(2,1)} %param.6) | copy-start | bytes 12582916
  423.7 27.9 %copy-start.6 = (f32[2048,128]{0,1:T(8,128)}, f32[2048,128]{0,1:T(8,128)S(1)}, u32[]{:S(2)}) copy-start(f32[2048,128]{0,1:T(8,128)S(1)} %fusion.30) | copy-start | bytes 3145732
  451.6 29.2 %all-to-all-start = ((f32[8,128,512]{2,1,0:T(8,128)}), f32[8,128,512]{2,1,0:T(8,128)}, u32[]{:S(2)}, u32[]{:S(2)}) async-start(f32[8,128,512]{2,1,0:T(8,128)} %bitcast.73), calls=%async_computation | async-start | bytes 4194304 | tf_op jit(solution)/shard_map/all_to_all | solution.py:28
  484.2 56.5 %all-to-all-start.1 = ((f32[8,128,512]{2,1,0:T(8,128)}), f32[8,128,512]{2,1,0:T(8,128)S(1)}, u32[]{:S(2)}, u32[]{:S(2)}) async-start(f32[8,128,512]{2,1,0:T(8,128)} %broadcast_in_dim.6), calls=%async_computation.1 | async-start | bytes 4194304 | tf_op jit(solution)/shard_map/all_to_all | solution.py:44
  489.9 52.2 %reduce-scatter.4.cloned.1.call-start = ((), (), s32[]{:S(2)}) async-start(), calls=%async_computation.8 | async-start | bytes 1179648
  494.6 156.8 %all-gather.5.cloned.1.call-start = ((), (), s32[]{:S(2)}) async-start(), calls=%async_computation.7 | async-start | bytes 17825792 | tf_op jit(solution)/shard_map/all_gather | solution.py:68
  540.7 4.8 copy-start.3
  542.1 148.1 %all-gather.3.cloned.1.call-start = ((), (), s32[]{:S(2)}) async-start(), calls=%async_computation.6 | async-start | bytes 1179648 | tf_op jit(solution)/shard_map/all_gather | solution.py:64
  690.2 5.0 copy-start.10
  695.2 2.4 copy-start.11
  697.6 39.1 %all-to-all-start.2 = ((f32[8,32,1024]{2,1,0:T(8,128)}), f32[8,32,1024]{2,1,0:T(8,128)}, u32[]{:S(2)}, u32[]{:S(2)}) async-start(f32[8,32,1024]{2,1,0:T(8,128)} %bitcast.17), calls=%async_computation.2 | async-start | bytes 2097152 | tf_op jit(solution)/shard_map/all_to_all | solution.py:28
  705.4 33.3 %copy-start.1 = (f32[1024,512]{1,0:T(8,128)S(1)}, f32[1024,512]{1,0:T(8,128)}, u32[]{:S(2)}) copy-start(f32[1024,512]{1,0:T(8,128)} %param.7) | copy-start | bytes 6291460
Sparse Core Ops, SparseCore 0:
  26.2 154.2 all-reduce.3
  192.3 76.5 all-reduce.5
  494.8 44.0 reduce-scatter.3
  542.2 109.1 all-gather.4
  653.4 36.7 all-gather.2
where the time goes:
time: 755 us; the launch traced here: 745 us
  waiting for transfers between devices  394 us (52%)
  other arithmetic  132 us (17%)
  matrix products  118 us (16%)
  blocking collectives  45.9 us (6%)
  starting transfers between devices  19.8 us (3%)
  local copies, waits for them, and re-layouts  18.4 us (2%)
  between operations  16.9 us (2%)
    psum x1, waiting for transfers between devices, per_device(): left_raw = lax.psum(partial_left, COL)  154 us
    all_gather x1, waiting for transfers between devices, from_root(): lax.all_gather(array, axis)  106 us
    another operation x14, other arithmetic, per_device(): factor = jnp.linalg.cholesky(gram_matrix)  78.7 us
    psum x1, waiting for transfers between devices, per_device(): gram_matrix = lax.psum(contract_first(left_raw, left_raw, highest), ROW)  76.7 us
    psum x5, blocking collectives, over_axes(): return functools.reduce(lax.psum, axes, array)  45.9 us
    another operation x4, other arithmetic, per_device(): lax.linalg.triangular_solve(factor, left_raw, left_side=False, lower=True...  42.5 us
    dot_general x2, matrix products, contract_first(): lax.dot_general(lhs, rhs, (((0,), (0,)), ((), ())), precision=highest, pr...  39.5 us
    all_gather x1, waiting for transfers between devices, spread(): lax.all_gather(own, axis, axis=0, tiled=True)[:len(lines)]  37.1 us
  transfers between devices with their start and end apart: 8, of which 5 were waited for; matrix products, arithmetic and copies ran while one was open for 6% of the time, Pallas kernels for 0%

commit v1 on v0

v1 whole, which is shorter than its diff:
```python
import jax
import jax.numpy as jnp
from jax import lax
from jax.sharding import Mesh
from jax.sharding import PartitionSpec as P

DIN = 16384
COL = ("col_0", "col_1", "col_2")
ROW = ("row_0", "row_1")
ALL = ROW + COL
CORE = "col_2"
CHIPS = ("col_0", "col_1")

decay_part = 0.05
step_size = 0.01
epsilon = 1e-06

HIGH = lax.Precision.HIGH
HIGHEST = lax.Precision.HIGHEST


def dot(lhs, rhs, dims, precision=None):
    return lax.dot_general(
        lhs, rhs, ((dims[:1], dims[1:]), ((), ())), precision=precision, preferred_element_type=jnp.float32
    )


def scatter_sum(array, axes, length):
    pieces = array.reshape(length, array.shape[0] // length, *array.shape[1:])
    return jnp.sum(lax.all_to_all(pieces, axes, 0, 0, tiled=True).astype(jnp.float32), axis=0)


def gathered(array, axes, length):
    pieces = lax.all_to_all(
        jnp.broadcast_to(array[None], (length, *array.shape)), axes, 0, 0, tiled=True
    )
    return pieces.reshape(length * array.shape[0], *array.shape[1:])


def to_other_core(array):
    return lax.ppermute(array, CORE, [(0, 1), (1, 0)])


def both_halves(own, core):
    other = to_other_core(own)
    return jnp.where(
        core == 0, jnp.concatenate([own, other], axis=0), jnp.concatenate([other, own], axis=0)
    )


def to_tile_owner(array):
    pairs = [(r * 16 + 2 * j + k, j * 16 + 2 * r + k) for r in range(8) for j in range(8) for k in range(2)]
    return lax.ppermute(array, ALL, pairs)


def per_device(momentum, gradient, right_prev, weight, tokens):
    core = lax.axis_index(CORE)
    mixed = momentum.astype(jnp.float32) + gradient.astype(jnp.float32)
    partial_left = dot(mixed, right_prev, (1, 0), HIGH)
    halves = partial_left.reshape(2, 1024, 512)
    sent = lax.dynamic_index_in_dim(halves, 1 - core, 0, keepdims=False)
    kept = lax.dynamic_index_in_dim(halves, core, 0, keepdims=False)
    left_shard = scatter_sum(kept + to_other_core(sent), CHIPS, 8)

    gram_partial = dot(left_shard, left_shard, (0, 0), HIGHEST)
    gram_matrix = gathered(scatter_sum(gram_partial, ALL, 128), ALL, 128)
    factor = jnp.linalg.cholesky(gram_matrix)
    inverse = lax.linalg.triangular_solve(
        factor, jnp.eye(512, dtype=jnp.float32), left_side=True, lower=True
    )

    left_rows = both_halves(gathered(left_shard, CHIPS, 8), core)
    partial_right = dot(mixed, left_rows, (0, 0), HIGH)
    right_shard = scatter_sum(partial_right, ROW, 8)
    tile_left_raw = gathered(to_tile_owner(left_shard), ROW, 8)
    tile_right_raw = to_tile_owner(right_shard)

    right_own = dot(right_shard, inverse, (1, 1), HIGHEST)
    squares = jnp.sum(gathered(jnp.sum(right_own * right_own, axis=0)[None], ALL, 128), axis=0)
    scale = lax.rsqrt(squares / DIN + epsilon)
    right_factor = gathered(right_own.astype(jnp.bfloat16), ROW, 8)
    new_basis = right_factor.astype(jnp.float32) * scale
    left_factor = dot(left_rows, inverse, (1, 1), HIGH).astype(jnp.bfloat16)
    outer = dot(left_factor, right_factor, (1, 1))
    new_momentum = (mixed - decay_part * outer).astype(jnp.bfloat16)

    tile_right = dot(tile_right_raw, inverse, (1, 1), HIGHEST).astype(jnp.bfloat16)
    tile_right = both_halves(gathered(tile_right, CHIPS, 8), core)
    tile_left = (dot(tile_left_raw, inverse, (1, 1), HIGH) * scale).astype(jnp.bfloat16)
    update = dot(tile_left, tile_right, (1, 1))
    new_weight = (weight.astype(jnp.float32) - step_size * update).astype(jnp.bfloat16)
    partial_projected = dot(tokens, new_weight, (1, 1)).astype(jnp.bfloat16)
    projected = scatter_sum(partial_projected, ROW, 8).astype(jnp.bfloat16)
    return (new_momentum, new_basis, new_weight, projected)


def solution(mesh):
    torus = Mesh(mesh.devices.reshape(4, 2, 4, 2, 2), ("row_0", "row_1", "col_0", "col_1", "col_2"))
    placed = (P(ROW, COL), P(ROW, COL), P(COL, None), P(COL, ROW), P(None, ROW))
    return jax.shard_map(
        per_device,
        mesh=torus,
        in_specs=placed,
        out_specs=(P(ROW, COL), P(COL, None), P(COL, ROW), P(ROW, COL)),
        check_vma=False,
    )
```

time: 755 us -> 453 us (0.60)
  waiting for transfers between devices: 394 us -> 101 us
  matrix products: 118 us -> 69 us
  starting transfers between devices: 19.8 us -> 54.7 us
  blocking collectives: 45.9 us -> 60.4 us
  between operations: 16.9 us -> 3.89 us
  local copies, waits for them, and re-layouts: 18.4 us -> 28.4 us
    psum x2 -> x0, waiting for transfers between devices: 231 us -> none  [the longest x1 154 us: per_device(): left_raw = lax.psum(partial_left, COL)]
    all_gather x2 -> x0, waiting for transfers between devices: 143 us -> none  [the longest x1 106 us: from_root(): lax.all_gather(array, axis)]
    all_to_all x3 -> x8, waiting for transfers between devices: 20.2 us -> 88 us  [the longest x6 88 us: gathered(): lax.all_to_all(jnp.broadcast_to(array[None], (length, *array.shape)), axe...]
    all_to_all x0 -> x2, blocking collectives: none -> 60.4 us  [scatter_sum(): lax.all_to_all(pieces, axes, 0, 0, tiled=True).astype(jnp.float32)]
    psum x5 -> x0, blocking collectives: 45.9 us -> none  [over_axes(): return functools.reduce(lax.psum, axes, array)]
    dot_general x6 -> x10, matrix products: 95.5 us -> 56.5 us  [dot(): lax.dot_general(lhs, rhs, ((dims[:1], dims[1:]), ((), ())), precision=pre...]
    all_to_all x3 -> x8, starting transfers between devices: 19.7 us -> 47.3 us  [the longest x6 36.7 us: gathered(): lax.all_to_all(jnp.broadcast_to(array[None], (length, *array.shape)), axe...]
    another operation x7, matrix products: 20.6 us -> 7.08 us  [per_device(): lax.linalg.triangular_solve(factor, jnp.eye(512, dtype=jnp.float32), left...]
  transfers between devices with their start and end apart: 8 -> 13, of which waited for: 5 -> 8; matrix products, arithmetic and copies ran while one was open for 6% -> 41% of each run, Pallas kernels for 0% -> 0%
where the time goes in v1:
time: 453 us; the launch traced here: 445 us
  other arithmetic  128 us (28%)
  waiting for transfers between devices  101 us (22%)
  matrix products  69 us (15%)
  blocking collectives  60.4 us (13%)
  starting transfers between devices  54.7 us (12%)
  local copies, waits for them, and re-layouts  28.4 us (6%)
    all_to_all x6, waiting for transfers between devices, gathered(): lax.all_to_all(jnp.broadcast_to(array[None], (length, *array.shape)), axe...  88 us
    another operation x14, other arithmetic, per_device(): factor = jnp.linalg.cholesky(gram_matrix)  78.7 us
    all_to_all x2, blocking collectives, scatter_sum(): lax.all_to_all(pieces, axes, 0, 0, tiled=True).astype(jnp.float32)  60.4 us
    dot_general x10, matrix products, dot(): lax.dot_general(lhs, rhs, ((dims[:1], dims[1:]), ((), ())), precision=pre...  56.5 us
    another operation x3, other arithmetic, per_device(): lax.linalg.triangular_solve(factor, jnp.eye(512, dtype=jnp.float32), left...  40.4 us
    all_to_all x6, starting transfers between devices, gathered(): lax.all_to_all(jnp.broadcast_to(array[None], (length, *array.shape)), axe...  36.7 us
    another operation x12, local copies, waits for them, and re-layouts  11.8 us
    all_to_all x2, starting transfers between devices, scatter_sum(): lax.all_to_all(pieces, axes, 0, 0, tiled=True).astype(jnp.float32)  10.5 us
  transfers between devices with their start and end apart: 13, of which 8 were waited for; matrix products, arithmetic and copies ran while one was open for 41% of the time, Pallas kernels for 0%

profile of v1, /device:TPU:2, one launch (start us, length us, event | category | flops | bytes accessed | tf_op | source)
XLA Modules:
  0.0 445.4 jit_solution(13762444178295398163)
XLA Ops:
  0.7 1.6 copy-done
  2.2 10.5 %fusion.1 = f32[2048,512]{1,0:T(8,128)} fusion(f32[1024,512]{1,0:T(8,128)S(1)} %copy-done, bf16[2048,1024]{1,0:T(8,128)(2,1)} %param.6, bf16[2048,1024]{1,0:T(8,128)(2,1)} %param.5), kind=kOutput, calls=%fused_computation.6 | convolution fusion | flops 6448742400 | bytes 14680064 | tf_op jit(solution)/shard_map/dot_general | solution.py:23
  12.7 3.1 dynamic-slice_bitcast_fusion
  15.8 4.4 collective-permute-done
  20.1 2.1 bitcast_add_fusion
  22.2 36.0 %all_to_all.50 = f32[8,128,512]{2,1,0:T(8,128)S(1)} all-to-all(f32[8,128,512]{2,1,0:T(8,128)S(1)} %bitcast.77), channel_id=1, replica_groups=mesh['row_0'=4,'row_1'=2,'col_0'=4,'col_1'=2,'col_2'=2] {'col_0','col_1'}, dimensions={0} | all-to-all | bytes 4194304 | tf_op jit(solution)/shard_map/all_to_all | solution.py:30
  58.5 1.0 fusion.21
  60.2 24.4 %all_to_all.51 = f32[128,4,512]{2,1,0:T(4,128)S(1)} all-to-all(f32[128,4,512]{2,1,0:T(4,128)S(1)} %copy.25), channel_id=1, replica_groups=mesh['row_0'=4,'row_1'=2,'col_0'=4,'col_1'=2,'col_2'=2] {'row_0','row_1'..., dimensions={0} | all-to-all | bytes 2097152 | tf_op jit(solution)/shard_map/all_to_all | solution.py:30
  84.6 1.6 broadcast_in_dim.14
  86.2 4.3 all-to-all-start.1
  90.8 30.0 %all-to-all-done.1 = f32[8,128,512]{2,1,0:T(8,128)} async-done(((f32[8,128,512]{2,1,0:T(8,128)}), f32[8,128,512]{2,1,0:T(8,128)}, u32[]{:S(2)}, u32[]{:S(2)}) %all-to-all-start.1) | async-done | bytes 2097184 | tf_op jit(solution)/shard_map/all_to_all | solution.py:34
  120.8 1.1 broadcast_in_dim.15
  121.9 6.9 %all-to-all-start.3 = ((f32[128,4,512]{2,1,0:T(4,128)}), f32[128,4,512]{2,1,0:T(4,128)S(1)}, u32[]{:S(2)}, u32[]{:S(2)}) async-start(f32[128,4,512]{2,1,0:T(4,128)} %broadcast_in_dim.15), calls=%async_computation.3 | async-start | bytes 2097152 | tf_op jit(solution)/shard_map/all_to_all | solution.py:34
  128.9 1.1 fusion.19
  130.7 16.9 %all-to-all-done.3 = f32[128,4,512]{2,1,0:T(4,128)S(1)} async-done(((f32[128,4,512]{2,1,0:T(4,128)}), f32[128,4,512]{2,1,0:T(4,128)S(1)}, u32[]{:S(2)}, u32[]{:S(2)}) %all-to-all-start.3) | async-done | bytes 1048608 | tf_op jit(solution)/shard_map/all_to_all | solution.py:34
  148.6 1.0 copy-done.3
  149.5 11.7 %cholesky.104 = f32[128,128]{1,0:T(8,128)S(1)} custom-call(f32[128,128]{1,0:T(8,128)S(1)} %cholesky.266), custom_call_target="Cholesky" | custom-call | tf_op jit(solution)/shard_map/jit(cholesky)/cholesky | solution.py:67
  161.4 9.8 %custom-call.30 = f32[1,128,128]{1,2,0:T(8,128)S(1)} custom-call(f32[1,128,128]{2,1,0:T(8,128)S(1)} %get-tuple-element.33), custom_call_target="InvertDiagBlocksLowerTriangular" | custom-call | tf_op jit(solution)/shard_map/jit(cholesky)/cholesky | solution.py:67
  171.2 1.2 constant_dynamic-update-slice_fusion.3
  172.5 1.3 convolution_subtract_fusion.3
  173.8 11.7 %cholesky.217 = f32[128,128]{1,0:T(8,128)S(1)} custom-call(f32[128,128]{1,0:T(8,128)S(1)} %cholesky.270), custom_call_target="Cholesky" | custom-call | tf_op jit(solution)/shard_map/jit(cholesky)/cholesky | solution.py:67
  185.5 10.0 %custom-call.31 = f32[1,128,128]{1,2,0:T(8,128)S(1)} custom-call(f32[1,128,128]{2,1,0:T(8,128)S(1)} %get-tuple-element.30), custom_call_target="InvertDiagBlocksLowerTriangular" | custom-call | tf_op jit(solution)/shard_map/jit(cholesky)/cholesky | solution.py:67
  195.7 1.3 convolution_subtract_fusion.4
  197.0 11.7 %cholesky.238 = f32[128,128]{1,0:T(8,128)S(1)} custom-call(f32[128,128]{1,0:T(8,128)S(1)} %cholesky.275), custom_call_target="Cholesky" | custom-call | tf_op jit(solution)/shard_map/jit(cholesky)/cholesky | solution.py:67
  208.8 9.8 %custom-call.32 = f32[1,128,128]{1,2,0:T(8,128)S(1)} custom-call(f32[1,128,128]{2,1,0:T(8,128)S(1)} %get-tuple-element.27), custom_call_target="InvertDiagBlocksLowerTriangular" | custom-call | tf_op jit(solution)/shard_map/jit(cholesky)/cholesky | solution.py:67
  218.8 1.2 convolution_subtract_fusion.5
  220.0 11.9 %cholesky.255 = f32[128,128]{1,0:T(8,128)S(1)} custom-call(f32[128,128]{1,0:T(8,128)S(1)} %convolution_subtract_fusion.5), custom_call_target="Cholesky" | custom-call | tf_op jit(solution)/shard_map/jit(cholesky)/cholesky | solution.py:67
  236.5 1.1 select_select_fusion
  237.6 13.9 %fusion = f32[1024,512]{1,0:T(8,128)} fusion(bf16[2048,1024]{1,0:T(8,128)(2,1)} %param.6, bf16[2048,1024]{1,0:T(8,128)(2,1)} %param.5, f32[1024,512]{1,0:T(8,128)} %collective-permute-done.1, f32[1024,512]{1,0:T(8,128)} %bitcast.4, pred[]{:T(512)S(6)} %eq.13), kind=kOutput, calls=%fused_computation.5 | convolution fusion | flops 6451888128 | bytes 14680065 | tf_op jit(solution)/shard_map/dot_general | solution.py:23
  251.5 4.8 %all-to-all-start.4 = ((f32[8,128,512]{2,1,0:T(8,128)}), f32[8,128,512]{2,1,0:T(8,128)S(1)}, u32[]{:S(2)}, u32[]{:S(2)}) async-start(f32[8,128,512]{2,1,0:T(8,128)} %bitcast.81), calls=%async_computation.4 | async-start | bytes 4194304 | tf_op jit(solution)/shard_map/all_to_all | solution.py:30
  256.4 11.9 %while.1 = (s32[]{:T(128)}, f32[512,512]{1,0:T(8,128)}, s32[4,2]{0,1:T(2,128)S(1)}, f32[4,128,128]{2,1,0:T(8,128)S(1)}, s32[]{:T(128)}) while((s32[]{:T(128)}, f32[512,512]{1,0:T(8,128)}, s32[4,2]{0,1:T(2,128)S(1)}, f32[4,128,128]{2,1,0:T(8,128)S(1)}, s32[]{:T(128)}) %tuple.34), condition=%wide.while_cond, body=%wide.while_body.sunk | while | flops 2 | bytes 131189 | solution.py:68
  257.0 2.3 bitcast_dynamic-update-slice_fusion.2
  260.0 2.3 bitcast_dynamic-update-slice_fusion.2
  263.0 2.3 bitcast_dynamic-update-slice_fusion.2
  266.0 2.2 bitcast_dynamic-update-slice_fusion.2
  268.2 39.3 %custom-call.33 = f32[4,128,128]{1,2,0:T(8,128)S(1)} custom-call(f32[4,128,128]{2,1,0:T(8,128)S(1)} %get-tuple-element.11), custom_call_target="InvertDiagBlocksLowerTriangular" | custom-call | tf_op jit(solution)/shard_map/triangular_solve | solution.py:68
  307.9 1.4 convolution_subtract_fusion.1
  309.7 1.5 convolution_subtract_fusion
  311.7 1.8 convolution_subtract_fusion.2
  314.4 2.1 collective-permute-start.3
  316.5 1.3 fusion.33
  317.8 2.2 multiply_reduce_fusion
  320.9 9.6 %all-to-all-start.6 = ((f32[128,1,512]{2,1,0:T(1,128)}), f32[128,1,512]{2,1,0:T(1,128)S(1)}, u32[]{:S(2)}, u32[]{:S(2)}) async-start(f32[128,1,512]{2,1,0:T(1,128)} %broadcast_in_dim.17), calls=%async_computation.6 | async-start | bytes 524288 | tf_op jit(solution)/shard_map/all_to_all | solution.py:34
  330.5 1.2 convolution_convert_fusion.2
  331.6 9.3 %all-to-all-done.6 = f32[128,1,512]{2,1,0:T(1,128)S(1)} async-done(((f32[128,1,512]{2,1,0:T(1,128)}), f32[128,1,512]{2,1,0:T(1,128)S(1)}, u32[]{:S(2)}, u32[]{:S(2)}) %all-to-all-start.6) | async-done | bytes 262176 | tf_op jit(solution)/shard_map/all_to_all | solution.py:34
  341.0 1.1 broadcast_in_dim.19
  342.0 4.0 all-to-all-start.8
  346.0 4.7 %collective-permute-start.2 = (f32[128,512]{1,0:T(8,128)S(1)}, f32[128,512]{1,0:T(8,128)S(1)}, u32[]{:S(2)}, u32[]{:S(2)}) collective-permute-start(f32[128,512]{1,0:T(8,128)S(1)} %reduce_sum.57), channel_id=1, source_target_pairs={{0,0},{1,1},{2,16},{3,17},{4,32},{5,33},{6,48},{7,49},{8,64},{9,65... | collective-permute-start | bytes 786440 | tf_op jit(solution)/shard_map/ppermute | solution.py:53
  350.7 9.0 %collective-permute-done.2 = f32[128,512]{1,0:T(8,128)S(1)} collective-permute-done((f32[128,512]{1,0:T(8,128)S(1)}, f32[128,512]{1,0:T(8,128)S(1)}, u32[]{:S(2)}, u32[]{:S(2)}) %collective-permute-start.2) | collective-permute-done | bytes 262176 | tf_op jit(solution)/shard_map/ppermute | solution.py:53
  359.7 12.0 %all-to-all-done.8 = bf16[8,128,512]{2,1,0:T(8,128)(2,1)S(1)} async-done(((bf16[8,128,512]{2,1,0:T(8,128)(2,1)}), bf16[8,128,512]{2,1,0:T(8,128)(2,1)S(1)}, u32[]{:S(2)}, u32[]{:S(2)}) %all-to-all-start.8) | async-done | bytes 1048608 | tf_op jit(solution)/shard_map/all_to_all | solution.py:34
  371.8 1.7 broadcast_in_dim.18
  373.4 5.9 %all-to-all-start.7 = ((f32[8,128,512]{2,1,0:T(8,128)}), f32[8,128,512]{2,1,0:T(8,128)S(1)}, u32[]{:S(2)}, u32[]{:S(2)}) async-start(f32[8,128,512]{2,1,0:T(8,128)} %broadcast_in_dim.18), calls=%async_computation.7 | async-start | bytes 4194304 | tf_op jit(solution)/shard_map/all_to_all | solution.py:34
  379.3 8.2 %convolution_convert_fusion = bf16[2048,512]{1,0:T(8,128)(2,1)} fusion(f32[1024,512]{1,0:T(8,128)} %collective-permute-done.1, f32[1024,512]{1,0:T(8,128)} %bitcast.4, pred[]{:T(512)S(6)} %eq.13, f32[128,512]{1,0:T(8,128)S(1)} %copy-done.8, f32[128,512]{1,0:T(8,128)S(1)} %fusion.34, f32[128,512]{1,0:T(8,128)S(1)} %fusion.36, f32[128,512]{1,0:T(8,128)S(1)} %fusion.24), kind=kOutput, calls=%fused_computation.8 | convolution fusion | flops 3226206208 | bytes 7340033 | tf_op jit(solution)/shard_map/dot_general | solution.py:23
  387.8 19.1 %all-to-all-done.7 = f32[8,128,512]{2,1,0:T(8,128)S(1)} async-done(((f32[8,128,512]{2,1,0:T(8,128)}), f32[8,128,512]{2,1,0:T(8,128)S(1)}, u32[]{:S(2)}, u32[]{:S(2)}) %all-to-all-start.7) | async-done | bytes 2097184 | tf_op jit(solution)/shard_map/all_to_all | solution.py:34
  406.9 1.1 broadcast_in_dim.16
  407.9 6.0 %all-to-all-start.5 = ((bf16[8,128,512]{2,1,0:T(8,128)(2,1)}), bf16[8,128,512]{2,1,0:T(8,128)(2,1)S(1)}, u32[]{:S(2)}, u32[]{:S(2)}) async-start(bf16[8,128,512]{2,1,0:T(8,128)(2,1)} %broadcast_in_dim.16), calls=%async_computation.5 | async-start | bytes 2097152 | tf_op jit(solution)/shard_map/all_to_all | solution.py:34
  414.0 3.0 multiply_convert_fusion
  417.0 5.4 %subtract_convert_fusion = bf16[1024,2048]{1,0:T(8,128)(2,1)S(1)} fusion(bf16[1024,2048]{1,0:T(8,128)(2,1)} %param.8, bf16[1024,512]{1,0:T(8,128)(2,1)S(1)} %multiply_convert_fusion, bf16[1024,512]{1,0:T(8,128)(2,1)} %collective-permute-done.4, bf16[1024,512]{1,0:T(8,128)(2,1)S(1)} %bitcast.83, pred[]{:T(512)S(6)} %eq.13), kind=kOutput, calls=%fused_computation.2 | convolution fusion | flops 2165309440 | bytes 11534337 | tf_op jit(solution)/shard_map/dot_general | solution.py:23
  422.4 2.0 copy-done.11
  424.4 2.1 convolution_convert_fusion.1
  427.2 5.7 %all-to-all-start.9 = ((bf16[8,32,1024]{2,1,0:T(8,128)(2,1)}), bf16[8,32,1024]{2,1,0:T(8,128)(2,1)}, u32[]{:S(2)}, u32[]{:S(2)}) async-start(bf16[8,32,1024]{2,1,0:T(8,128)(2,1)} %bitcast.24), calls=%async_computation.9 | async-start | bytes 1048576 | tf_op jit(solution)/shard_map/all_to_all | solution.py:30
  432.9 8.9 %subtract_convert_fusion.1 = bf16[2048,1024]{1,0:T(8,128)(2,1)} fusion(bf16[2048,1024]{1,0:T(8,128)(2,1)} %param.6, bf16[2048,1024]{1,0:T(8,128)(2,1)} %param.5, bf16[2048,512]{1,0:T(8,128)(2,1)} %convolution_convert_fusion, bf16[1024,512]{1,0:T(8,128)(2,1)S(1)} %bitcast.80), kind=kOutput, calls=%fused_computation.3 | convolution fusion | flops 2160066560 | bytes 15728640 | tf_op jit(solution)/shard_map/dot_general | solution.py:23
  441.8 1.7 convert_multiply_fusion
  443.5 1.8 reduce_sum.62
  (69 shorter events, 12.1 us)
Async XLA Ops:
  0.6 1.6 copy-start
  15.8 4.4 collective-permute-start
  86.2 34.5 %all-to-all-start.1 = ((f32[8,128,512]{2,1,0:T(8,128)}), f32[8,128,512]{2,1,0:T(8,128)}, u32[]{:S(2)}, u32[]{:S(2)}) async-start(f32[8,128,512]{2,1,0:T(8,128)} %broadcast_in_dim.14), calls=%async_computation.1 | async-start | bytes 4194304 | tf_op jit(solution)/shard_map/all_to_all | solution.py:34
  121.9 25.7 %all-to-all-start.3 = ((f32[128,4,512]{2,1,0:T(4,128)}), f32[128,4,512]{2,1,0:T(4,128)S(1)}, u32[]{:S(2)}, u32[]{:S(2)}) async-start(f32[128,4,512]{2,1,0:T(4,128)} %broadcast_in_dim.15), calls=%async_computation.3 | async-start | bytes 2097152 | tf_op jit(solution)/shard_map/all_to_all | solution.py:34
  130.0 107.6 %collective-permute-start.1 = (f32[1024,512]{1,0:T(8,128)}, f32[1024,512]{1,0:T(8,128)}, u32[]{:S(2)}, u32[]{:S(2)}) collective-permute-start(f32[1024,512]{1,0:T(8,128)} %bitcast.4), channel_id=1, source_target_pairs={{0,1},{1,0},{2,3},{3,2},{4,5},{5,4},{6,7},{7,6},{8,9},{9,8},{10,11... | collective-permute-start | bytes 6291464 | tf_op jit(solution)/shard_map/ppermute | solution.py:41
  148.6 1.0 copy-start.3
  251.5 61.9 %all-to-all-start.4 = ((f32[8,128,512]{2,1,0:T(8,128)}), f32[8,128,512]{2,1,0:T(8,128)S(1)}, u32[]{:S(2)}, u32[]{:S(2)}) async-start(f32[8,128,512]{2,1,0:T(8,128)} %bitcast.81), calls=%async_computation.4 | async-start | bytes 4194304 | tf_op jit(solution)/shard_map/all_to_all | solution.py:30
  307.6 3.7 copy-start.9
  309.7 77.9 %copy-start.2 = (f32[128,512]{1,0:T(8,128)}, f32[128,512]{1,0:T(8,128)S(1)}, u32[]{:S(2)}) copy-start(f32[128,512]{1,0:T(8,128)S(1)} %fusion.36) | copy-start | bytes 786436
  311.7 67.6 %copy-start.4 = (f32[128,512]{1,0:T(8,128)}, f32[128,512]{1,0:T(8,128)S(1)}, u32[]{:S(2)}) copy-start(f32[128,512]{1,0:T(8,128)S(1)} %fusion.34) | copy-start | bytes 786436
  314.4 16.1 %collective-permute-start.3 = (f32[128,512]{1,0:T(8,128)}, f32[128,512]{1,0:T(8,128)S(1)}, u32[]{:S(2)}, u32[]{:S(2)}) collective-permute-start(f32[128,512]{1,0:T(8,128)} %reduce_sum.59), channel_id=1, source_target_pairs={{0,0},{1,1},{2,16},{3,17},{4,32},{5,33},{6,48},{7,49},{8,64},{9,65... | collective-permute-start | bytes 786440 | tf_op jit(solution)/shard_map/ppermute | solution.py:53
  317.8 24.3 %copy-start.7 = (f32[128,512]{1,0:T(8,128)}, f32[128,512]{1,0:T(8,128)S(1)}, u32[]{:S(2)}) copy-start(f32[128,512]{1,0:T(8,128)S(1)} %fusion.33) | copy-start | bytes 786436
  320.9 20.1 %all-to-all-start.6 = ((f32[128,1,512]{2,1,0:T(1,128)}), f32[128,1,512]{2,1,0:T(1,128)S(1)}, u32[]{:S(2)}, u32[]{:S(2)}) async-start(f32[128,1,512]{2,1,0:T(1,128)} %broadcast_in_dim.17), calls=%async_computation.6 | async-start | bytes 524288 | tf_op jit(solution)/shard_map/all_to_all | solution.py:34
  342.0 29.7 %all-to-all-start.8 = ((bf16[8,128,512]{2,1,0:T(8,128)(2,1)}), bf16[8,128,512]{2,1,0:T(8,128)(2,1)S(1)}, u32[]{:S(2)}, u32[]{:S(2)}) async-start(bf16[8,128,512]{2,1,0:T(8,128)(2,1)} %broadcast_in_dim.19), calls=%async_computation.8 | async-start | bytes 2097152 | tf_op jit(solution)/shard_map/all_to_all | solution.py:34
  346.0 13.7 %collective-permute-start.2 = (f32[128,512]{1,0:T(8,128)S(1)}, f32[128,512]{1,0:T(8,128)S(1)}, u32[]{:S(2)}, u32[]{:S(2)}) collective-permute-start(f32[128,512]{1,0:T(8,128)S(1)} %reduce_sum.57), channel_id=1, source_target_pairs={{0,0},{1,1},{2,16},{3,17},{4,32},{5,33},{6,48},{7,49},{8,64},{9,65... | collective-permute-start | bytes 786440 | tf_op jit(solution)/shard_map/ppermute | solution.py:53
  359.7 19.6 %copy-start.8 = (f32[128,512]{1,0:T(8,128)S(1)}, f32[128,512]{1,0:T(8,128)}, u32[]{:S(2)}) copy-start(f32[128,512]{1,0:T(8,128)} %copy-done.7) | copy-start | bytes 786436
  371.8 1.7 copy-start.5
  373.4 33.4 %all-to-all-start.7 = ((f32[8,128,512]{2,1,0:T(8,128)}), f32[8,128,512]{2,1,0:T(8,128)S(1)}, u32[]{:S(2)}, u32[]{:S(2)}) async-start(f32[8,128,512]{2,1,0:T(8,128)} %broadcast_in_dim.18), calls=%async_computation.7 | async-start | bytes 4194304 | tf_op jit(solution)/shard_map/all_to_all | solution.py:34
  379.3 37.7 %collective-permute-start.4 = (bf16[1024,512]{1,0:T(8,128)(2,1)}, bf16[1024,512]{1,0:T(8,128)(2,1)}, u32[]{:S(2)}, u32[]{:S(2)}) collective-permute-start(bf16[1024,512]{1,0:T(8,128)(2,1)} %bitcast.82), channel_id=1, source_target_pairs={{0,1},{1,0},{2,3},{3,2},{4,5},{5,4},{6,7},{7,6},{8,9},{9,8},{10,11... | collective-permute-start | bytes 3145736 | tf_op jit(solution)/shard_map/ppermute | solution.py:41
  407.9 19.2 %all-to-all-start.5 = ((bf16[8,128,512]{2,1,0:T(8,128)(2,1)}), bf16[8,128,512]{2,1,0:T(8,128)(2,1)S(1)}, u32[]{:S(2)}, u32[]{:S(2)}) async-start(bf16[8,128,512]{2,1,0:T(8,128)(2,1)} %broadcast_in_dim.16), calls=%async_computation.5 | async-start | bytes 2097152 | tf_op jit(solution)/shard_map/all_to_all | solution.py:34
  414.0 3.1 copy-start.6
  417.0 7.4 %copy-start.10 = (bf16[256,2048]{1,0:T(8,128)(2,1)S(1)}, bf16[256,2048]{1,0:T(8,128)(2,1)}, u32[]{:S(2)}) copy-start(bf16[256,2048]{1,0:T(8,128)(2,1)} %param.9) | copy-start | bytes 3145732
  422.4 2.0 copy-start.11
  427.2 16.3 %all-to-all-start.9 = ((bf16[8,32,1024]{2,1,0:T(8,128)(2,1)}), bf16[8,32,1024]{2,1,0:T(8,128)(2,1)}, u32[]{:S(2)}, u32[]{:S(2)}) async-start(bf16[8,32,1024]{2,1,0:T(8,128)(2,1)} %bitcast.24), calls=%async_computation.9 | async-start | bytes 1048576 | tf_op jit(solution)/shard_map/all_to_all | solution.py:30
  432.9 12.4 %copy-start.1 = (f32[1024,512]{1,0:T(8,128)S(1)}, f32[1024,512]{1,0:T(8,128)}, u32[]{:S(2)}) copy-start(f32[1024,512]{1,0:T(8,128)} %param.7) | copy-start | bytes 6291460
